TPU v7x, 32 devices: a whole 2x2x4 slice. The times are simulated.
32 devices in a mesh: rep: 4 (over x, core), shard: 8 (over z, y).
Axes of the slice: x: 2, y: 2, z: 4, core: 2. Of those that a mesh axis runs over, the one named last changes fastest.
Arguments:
- tokens: bfloat16 [4096, 768], P(('rep', 'shard')), may hold values from -6 to 6
- segment_ids: int32 [4096], P(('rep', 'shard')), may hold values from 0 to 3, as said below
- cotangent: bfloat16 [4096, 768], P(('rep', 'shard')), may hold values from -6 to 6
- ln1_gain: bfloat16 [1, 768], P(None, 'shard'), may hold values from 0.25 to 1.75
- ln1_bias: bfloat16 [1, 768], P(None, 'shard'), may hold values from -3 to 3
- qkv_weight: bfloat16 [1, 768, 2304], P(None, 'shard'), may hold values from -0.21875 to 0.21875
- qv_bias: bfloat16 [1, 1536], P(None, 'shard'), may hold values from -3 to 3
- out_weight: bfloat16 [1, 768, 768], P(None, 'shard'), may hold values from -0.875 to 0.875
- out_bias: bfloat16 [1, 768], P(None, 'shard'), may hold values from -3 to 3
- ln2_gain: bfloat16 [1, 768], P(None, 'shard'), may hold values from 0.25 to 1.75
- ln2_bias: bfloat16 [1, 768], P(None, 'shard'), may hold values from -3 to 3
- fc_weight: bfloat16 [1, 768, 3072], P(None, 'shard'), may hold values from -0.21875 to 0.21875
- fc_bias: bfloat16 [1, 3072], P(None, 'shard'), may hold values from -3 to 3
- proj_weight: bfloat16 [1, 3072, 768], P(None, 'shard'), may hold values from -0.109375 to 0.109375
- proj_bias: bfloat16 [1, 768], P(None, 'shard'), may hold values from -3 to 3
Outputs:
- out_tokens: bfloat16 [4096, 768], P(('rep', 'shard'))
- input_grad: float32 [4096, 768], P(('rep', 'shard'))
- grad_ln1_gain: float32 [1, 768], P(None, 'shard')
- grad_ln1_bias: float32 [1, 768], P(None, 'shard')
- grad_qkv_weight: float32 [1, 768, 2304], P(None, 'shard')
- grad_qv_bias: float32 [1, 1536], P(None, 'shard')
- grad_out_weight: float32 [1, 768, 768], P(None, 'shard')
- grad_out_bias: float32 [1, 768], P(None, 'shard')
- grad_ln2_gain: float32 [1, 768], P(None, 'shard')
- grad_ln2_bias: float32 [1, 768], P(None, 'shard')
- grad_fc_weight: float32 [1, 768, 3072], P(None, 'shard')
- grad_fc_bias: float32 [1, 3072], P(None, 'shard')
- grad_proj_weight: float32 [1, 3072, 768], P(None, 'shard')
- grad_proj_bias: float32 [1, 768], P(None, 'shard')
Inputs may be any that keep to these rules, and one draw needn't show every extreme that they name: `segment_ids`: each aligned block of 128 rows (one device's rows) holds three documents with ids 0, 1, 2 in this order, each of one row or more, followed by padding rows of id 3, which attend among themselves; the first block has no padding and the last block is half padding.
All inputs are finite; a program needn't handle non-finite values.
Results may differ from a plain program's by a relative error of at most 0.0098.
Values may be sent and summed in bfloat16 or wider, within the bound.
A program may use at most 128 MiB of HBM per device.

v0:
```python
import jax
import jax.numpy as jnp
from jax import lax
from jax.sharding import PartitionSpec as P

HEADS = 12
HEAD = 64
LAYERS = 1
epsilon = 1e-05


def to_float(value):
    return value.astype(jnp.float32)


def layer_norm(inputs, norm_gain, norm_shift):
    center = inputs - jnp.mean(inputs, axis=-1, keepdims=True)
    inverse_std = lax.rsqrt(jnp.mean(center * center, axis=-1, keepdims=True) + epsilon)
    normed = center * inverse_std
    return (normed * norm_gain + norm_shift, normed, inverse_std)


def norm_back(upstream, normed, inverse_std, norm_gain):
    scaled = upstream * norm_gain
    inner_term = scaled - jnp.mean(scaled, axis=-1, keepdims=True)
    inner_term = inner_term - normed * jnp.mean(scaled * normed, axis=-1, keepdims=True)
    return (inverse_std * inner_term, jnp.sum(upstream * normed, axis=0), jnp.sum(upstream, axis=0))


def layer_forward(inputs, allowed, weights, kept_lse):
    (
        ln1_gain,
        ln1_bias,
        qkv_weight,
        qv_bias,
        out_weight,
        out_bias,
        ln2_gain,
        ln2_bias,
        fc_weight,
        fc_bias,
        proj_weight,
        proj_bias,
    ) = weights
    row_count = inputs.shape[0]
    width_all = inputs.shape[1]
    first_norm, normed_one, inverse_one = layer_norm(inputs, to_float(ln1_gain), to_float(ln1_bias))
    first_low = first_norm.astype(jnp.bfloat16)
    offset = jnp.concatenate(
        [
            to_float(qv_bias[:width_all]),
            jnp.zeros((width_all,), jnp.float32),
            to_float(qv_bias[width_all:]),
        ]
    )
    projected = (
        jnp.dot(first_low, qkv_weight, preferred_element_type=jnp.float32) + offset
    ).astype(jnp.bfloat16)
    queries = projected[:, :width_all].reshape(row_count, HEADS, HEAD)
    keys_all = projected[:, width_all : 2 * width_all].reshape(row_count, HEADS, HEAD)
    values_all = projected[:, 2 * width_all :].reshape(row_count, HEADS, HEAD)
    scores = jnp.einsum(
        "qhd,khd->hqk", queries, keys_all, preferred_element_type=jnp.float32
    ) * HEAD ** (-0.5)
    scores = jnp.where(allowed[None], scores, -1e30)
    if kept_lse is None:
        row_max = jnp.max(scores, axis=-1, keepdims=True)
        log_total = row_max + jnp.log(jnp.sum(jnp.exp(scores - row_max), axis=-1, keepdims=True))
    else:
        log_total = kept_lse
    attn_probs = jnp.exp(scores - log_total)
    probs_low = attn_probs.astype(jnp.bfloat16)
    attn_mixed = jnp.einsum(
        "hqk,khd->qhd", probs_low, values_all, preferred_element_type=jnp.float32
    )
    attn_mixed = attn_mixed.reshape(row_count, width_all).astype(jnp.bfloat16)
    after_attn = (
        inputs
        + jnp.dot(attn_mixed, out_weight, preferred_element_type=jnp.float32)
        + to_float(out_bias)
    )
    second_norm, normed_two, inverse_two = layer_norm(
        after_attn, to_float(ln2_gain), to_float(ln2_bias)
    )
    second_low = second_norm.astype(jnp.bfloat16)
    hidden_pre = jnp.dot(second_low, fc_weight, preferred_element_type=jnp.float32) + to_float(
        fc_bias
    )
    hidden_low = jax.nn.gelu(hidden_pre, approximate=True).astype(jnp.bfloat16)
    result = (
        after_attn
        + jnp.dot(hidden_low, proj_weight, preferred_element_type=jnp.float32)
        + to_float(proj_bias)
    )
    return dict(
        normed_one=normed_one,
        inverse_one=inverse_one,
        first_low=first_low,
        queries=queries,
        keys_all=keys_all,
        values_all=values_all,
        attn_probs=attn_probs,
        probs_low=probs_low,
        attn_mixed=attn_mixed,
        normed_two=normed_two,
        inverse_two=inverse_two,
        second_low=second_low,
        hidden_pre=hidden_pre,
        hidden_low=hidden_low,
        result=result,
        log_total=log_total,
    )


def layer_backward(upstream, saved, weights):
    (
        ln1_gain,
        ln1_bias,
        qkv_weight,
        qv_bias,
        out_weight,
        out_bias,
        ln2_gain,
        ln2_bias,
        fc_weight,
        fc_bias,
        proj_weight,
        proj_bias,
    ) = weights
    row_count = upstream.shape[0]
    width_all = upstream.shape[1]
    proj_in = upstream.astype(jnp.bfloat16)
    grad_proj = jnp.einsum(
        "tf,td->fd", saved["hidden_low"], proj_in, preferred_element_type=jnp.float32
    )
    grad_proj_b = jnp.sum(to_float(proj_in), axis=0)
    hidden_grad = jnp.einsum("td,fd->tf", proj_in, proj_weight, preferred_element_type=jnp.float32)
    _, gelu_pull = jax.vjp(lambda value: jax.nn.gelu(value, approximate=True), saved["hidden_pre"])
    pre_grad = gelu_pull(hidden_grad)[0].astype(jnp.bfloat16)
    grad_fc = jnp.einsum(
        "td,tf->df", saved["second_low"], pre_grad, preferred_element_type=jnp.float32
    )
    grad_fc_b = jnp.sum(to_float(pre_grad), axis=0)
    second_grad = jnp.einsum("tf,df->td", pre_grad, fc_weight, preferred_element_type=jnp.float32)
    norm_part, grad_ln2_g, grad_ln2_b = norm_back(
        second_grad, saved["normed_two"], saved["inverse_two"], to_float(ln2_gain)
    )
    residual_grad = upstream + norm_part
    branch_in = residual_grad.astype(jnp.bfloat16)
    grad_out = jnp.einsum(
        "tc,td->cd", saved["attn_mixed"], branch_in, preferred_element_type=jnp.float32
    )
    grad_out_b = jnp.sum(to_float(branch_in), axis=0)
    mixed_grad = jnp.einsum("td,cd->tc", branch_in, out_weight, preferred_element_type=jnp.float32)
    mixed_grad = mixed_grad.astype(jnp.bfloat16).reshape(row_count, HEADS, HEAD)
    prob_grad = jnp.einsum(
        "qhd,khd->hqk", mixed_grad, saved["values_all"], preferred_element_type=jnp.float32
    )
    value_grad = jnp.einsum(
        "hqk,qhd->khd", saved["probs_low"], mixed_grad, preferred_element_type=jnp.float32
    )
    attn_probs = saved["attn_probs"]
    row_delta = jnp.sum(attn_probs * prob_grad, axis=-1, keepdims=True)
    score_grad = (attn_probs * (prob_grad - row_delta)).astype(jnp.bfloat16)
    query_grad = jnp.einsum(
        "hqk,khd->qhd", score_grad, saved["keys_all"], preferred_element_type=jnp.float32
    ) * HEAD ** (-0.5)
    key_grad = jnp.einsum(
        "hqk,qhd->khd", score_grad, saved["queries"], preferred_element_type=jnp.float32
    ) * HEAD ** (-0.5)
    joined_grad = jnp.concatenate(
        [
            query_grad.reshape(row_count, width_all),
            key_grad.reshape(row_count, width_all),
            value_grad.reshape(row_count, width_all),
        ],
        axis=1,
    ).astype(jnp.bfloat16)
    grad_qkv = jnp.einsum(
        "tc,te->ce", saved["first_low"], joined_grad, preferred_element_type=jnp.float32
    )
    column_sums = jnp.sum(to_float(joined_grad), axis=0)
    grad_qv_b = jnp.concatenate([column_sums[:width_all], column_sums[2 * width_all :]])
    first_grad = jnp.einsum(
        "te,ce->tc", joined_grad, qkv_weight, preferred_element_type=jnp.float32
    )
    norm_first, grad_ln1_g, grad_ln1_b = norm_back(
        first_grad, saved["normed_one"], saved["inverse_one"], to_float(ln1_gain)
    )
    gradients = (
        grad_ln1_g,
        grad_ln1_b,
        grad_qkv,
        grad_qv_b,
        grad_out,
        grad_out_b,
        grad_ln2_g,
        grad_ln2_b,
        grad_fc,
        grad_fc_b,
        grad_proj,
        grad_proj_b,
    )
    return (residual_grad + norm_first, gradients)


def own_grads(gradients):
    shares = (
        lax.psum_scatter(gradients[0], "shard", scatter_dimension=0, tiled=True),
        lax.psum_scatter(gradients[1], "shard", scatter_dimension=0, tiled=True),
        lax.psum_scatter(gradients[2], "shard", scatter_dimension=0, tiled=True),
        lax.psum_scatter(gradients[3], "shard", scatter_dimension=0, tiled=True),
        lax.psum_scatter(gradients[4], "shard", scatter_dimension=0, tiled=True),
        lax.psum_scatter(gradients[5], "shard", scatter_dimension=0, tiled=True),
        lax.psum_scatter(gradients[6], "shard", scatter_dimension=0, tiled=True),
        lax.psum_scatter(gradients[7], "shard", scatter_dimension=0, tiled=True),
        lax.psum_scatter(gradients[8], "shard", scatter_dimension=0, tiled=True),
        lax.psum_scatter(gradients[9], "shard", scatter_dimension=0, tiled=True),
        lax.psum_scatter(gradients[10], "shard", scatter_dimension=0, tiled=True),
        lax.psum_scatter(gradients[11], "shard", scatter_dimension=0, tiled=True),
    )
    owned = lax.psum(
        (
            shares[0],
            shares[1],
            shares[2],
            shares[3],
            shares[4],
            shares[5],
            shares[6],
            shares[7],
            shares[8],
            shares[9],
            shares[10],
            shares[11],
        ),
        "rep",
    )
    return owned


def per_device(
    tokens,
    segment_ids,
    cotangent,
    ln1_gain,
    ln1_bias,
    qkv_weight,
    qv_bias,
    out_weight,
    out_bias,
    ln2_gain,
    ln2_bias,
    fc_weight,
    fc_bias,
    proj_weight,
    proj_bias,
):
    row_count = tokens.shape[0]
    positions = jnp.arange(row_count)
    allowed = (segment_ids[:, None] == segment_ids[None, :]) & (
        positions[None, :] <= positions[:, None]
    )
    residual = to_float(tokens)
    layer_index = 0
    gathered = (
        lax.all_gather(ln1_gain[layer_index], "shard", axis=0, tiled=True),
        lax.all_gather(ln1_bias[layer_index], "shard", axis=0, tiled=True),
        lax.all_gather(qkv_weight[layer_index], "shard", axis=0, tiled=True),
        lax.all_gather(qv_bias[layer_index], "shard", axis=0, tiled=True),
        lax.all_gather(out_weight[layer_index], "shard", axis=0, tiled=True),
        lax.all_gather(out_bias[layer_index], "shard", axis=0, tiled=True),
        lax.all_gather(ln2_gain[layer_index], "shard", axis=0, tiled=True),
        lax.all_gather(ln2_bias[layer_index], "shard", axis=0, tiled=True),
        lax.all_gather(fc_weight[layer_index], "shard", axis=0, tiled=True),
        lax.all_gather(fc_bias[layer_index], "shard", axis=0, tiled=True),
        lax.all_gather(proj_weight[layer_index], "shard", axis=0, tiled=True),
        lax.all_gather(proj_bias[layer_index], "shard", axis=0, tiled=True),
    )
    saved = layer_forward(residual, allowed, gathered, None)
    kept_inputs = [residual]
    kept_lse = [saved["log_total"]]
    residual = saved["result"]
    out_tokens = residual.astype(jnp.bfloat16)
    upstream = to_float(cotangent)
    owned_grads = [None] * LAYERS
    for layer_index in reversed(range(LAYERS)):
        gathered = (
            lax.all_gather(ln1_gain[layer_index], "shard", axis=0, tiled=True),
            lax.all_gather(ln1_bias[layer_index], "shard", axis=0, tiled=True),
            lax.all_gather(qkv_weight[layer_index], "shard", axis=0, tiled=True),
            lax.all_gather(qv_bias[layer_index], "shard", axis=0, tiled=True),
            lax.all_gather(out_weight[layer_index], "shard", axis=0, tiled=True),
            lax.all_gather(out_bias[layer_index], "shard", axis=0, tiled=True),
            lax.all_gather(ln2_gain[layer_index], "shard", axis=0, tiled=True),
            lax.all_gather(ln2_bias[layer_index], "shard", axis=0, tiled=True),
            lax.all_gather(fc_weight[layer_index], "shard", axis=0, tiled=True),
            lax.all_gather(fc_bias[layer_index], "shard", axis=0, tiled=True),
            lax.all_gather(proj_weight[layer_index], "shard", axis=0, tiled=True),
            lax.all_gather(proj_bias[layer_index], "shard", axis=0, tiled=True),
        )
        saved = layer_forward(kept_inputs[layer_index], allowed, gathered, kept_lse[layer_index])
        upstream, gradients = layer_backward(upstream, saved, gathered)
        owned_grads[layer_index] = own_grads(gradients)
    stacked = tuple((jnp.stack([owned_grads[0][member]]) for member in range(12)))
    return (out_tokens, upstream) + stacked


def solution(mesh):
    placed = (
        P(("rep", "shard"), None),
        P(("rep", "shard")),
        P(("rep", "shard"), None),
        P(None, "shard"),
        P(None, "shard"),
        P(None, "shard", None),
        P(None, "shard"),
        P(None, "shard", None),
        P(None, "shard"),
        P(None, "shard"),
        P(None, "shard"),
        P(None, "shard", None),
        P(None, "shard"),
        P(None, "shard", None),
        P(None, "shard"),
    )
    return jax.shard_map(
        per_device,
        mesh=mesh,
        in_specs=placed,
        out_specs=(
            P(("rep", "shard"), None),
            P(("rep", "shard"), None),
            P(None, "shard"),
            P(None, "shard"),
            P(None, "shard", None),
            P(None, "shard"),
            P(None, "shard", None),
            P(None, "shard"),
            P(None, "shard"),
            P(None, "shard"),
            P(None, "shard", None),
            P(None, "shard"),
            P(None, "shard", None),
            P(None, "shard"),
        ),
        check_vma=False,
    )
```

profile of v0, /device:TPU:0, one launch (start us, length us, event | category | flops | bytes accessed | tf_op | source)
XLA Modules:
  0.0 913.5 jit_solution(14599363228877090021)
XLA Ops:
  13.7 39.5 %all-reduce.18 = (bf16[1536]{0:T(1024)(128)(2,1)S(1)}, bf16[768]{0:T(1024)(128)(2,1)S(1)}, bf16[768]{0:T(1024)(128)(2,1)S(1)}, bf16[768]{0:T(1024)(128)(2,1)S(1)...) all-reduce(bf16[1536]{0:T(1024)(128)(2,1)S(1)} %dynamic-update-slic, ...), channel_id=5, replica_groups=mesh['rep'=4,'shard'=8] {'shard'}, use_global_device_ids=true, to_apply=%add.2 | all-reduce | flops 6144 | bytes 24576
  53.3 26.1 %all-gather.9 = bf16[1,3072]{1,0:T(2,128)(2,1)S(1)} all-gather(bf16[1,384]{1,0:T(2,128)(2,1)S(1)} %copy-done.39), channel_id=11, replica_groups=mesh['rep'=4,'shard'=8] {'shard'}, dimensions={1}, use_global_device_ids=true | all-gather | bytes 6912 | tf_op jit(solution)/shard_map/all_gather | solution.py:276
  80.0 2.7 fusion.11
  84.0 36.8 %all-gather.19.cloned.1.call-done = bf16[1,768,768]{2,1,0:T(8,128)(2,1)} async-done(((bf16[1,96,768]{2,1,0:T(8,128)(2,1)}), bf16[1,768,768]{2,1,0:T(8,128)(2,1)}) %all-gather.19.cloned.1.call-update) | async-done | bytes 1179664 | tf_op jit(solution)/shard_map/all_gather | solution.py:271
  122.8 78.9 %all-gather.21.cloned.1.call-done = bf16[1,768,3072]{2,1,0:T(8,128)(2,1)} async-done(((bf16[1,96,3072]{2,1,0:T(8,128)(2,1)}), bf16[1,768,3072]{2,1,0:T(8,128)(2,1)}) %all-gather.21.cloned.1.call-update) | async-done | bytes 4718608 | tf_op jit(solution)/shard_map/all_gather | solution.py:275
  201.7 3.2 fusion.8
  204.9 76.8 %all-gather.23.cloned.1.call-done = bf16[1,3072,768]{2,1,0:T(8,128)(2,1)} async-done(((bf16[1,384,768]{2,1,0:T(8,128)(2,1)}), bf16[1,3072,768]{2,1,0:T(8,128)(2,1)}) %all-gather.23.cloned.1.call-update) | async-done | bytes 4718608 | tf_op jit(solution)/shard_map/all_gather | solution.py:277
  281.8 5.0 convert_reduce_fusion
  286.9 2.3 multiply_reduce_fusion.1
  290.7 1.8 fusion.63
  292.8 2.5 fusion.35
  295.3 1.7 copy.53
  300.2 4.1 fusion.66
  305.5 5.8 fusion.69
  312.2 5.2 fusion.70
  320.9 4.1 fusion.56
  324.9 35.8 %all-reduce.15 = (f32[768]{0:T(1024)S(1)}, f32[768]{0:T(1024)S(1)}, f32[1536]{0:T(1024)S(1)}, f32[768]{0:T(1024)S(1)}, f32[768]{0:T(1024)S(1)}, /*index=5*/f32[7...) all-reduce(f32[768]{0:T(1024)} %get-tuple-element.16, ...), channel_id=14, replica_groups=mesh['rep'=4,'shard'=8] {'shard'}, use_global_device_ids=true, to_apply=%region_12.13.clone | all-reduce | flops 9216 | bytes 73728
  360.8 130.8 %reduce-scatter.5.cloned.1.call-done = f32[96,2304]{1,0:T(8,128)} async-done(((f32[768,2304]{1,0:T(8,128)}), f32[96,2304]{1,0:T(8,128)}) %reduce-scatter.5.cloned.1.call-update) | async-done | bytes 884752 | tf_op jit(solution)/shard_map/reduce_scatter | solution.py:211
  491.5 166.6 %reduce-scatter.9.cloned.1.call-done = f32[96,3072]{1,0:T(8,128)} async-done(((f32[768,3072]{1,0:T(8,128)}), f32[96,3072]{1,0:T(8,128)}) %reduce-scatter.9.cloned.1.call-update) | async-done | bytes 1179664 | tf_op jit(solution)/shard_map/reduce_scatter | solution.py:217
  658.1 166.6 %reduce-scatter.11.cloned.1.call-done = f32[384,768]{1,0:T(8,128)} async-done(((f32[3072,768]{1,0:T(8,128)}), f32[384,768]{1,0:T(8,128)}) %reduce-scatter.11.cloned.1.call-update) | async-done | bytes 1179664 | tf_op jit(solution)/shard_map/reduce_scatter | solution.py:219
  825.3 7.5 all-reduce.16
  833.8 4.1 fusion.38
  837.9 64.1 %all-reduce.21.cloned.1.call-done = (f32[1,96,2304]{2,1,0:T(8,128)}, f32[1,96,768]{2,1,0:T(8,128)}, f32[1,96,3072]{2,1,0:T(8,128)}, f32[1,384,768]{2,1,0:T(8,128)}) async-done(((f32[1,96,2304]{2,1,0:T(8,128)}, f32[1,96,768]{2,1,0:T(8,128)}, f32[1,96,3072]{2,1,0:T(8,128)}, f32[1,384,768]{2,1,0:T(8,128)}), (f32[1,96,2304]{2,1,0:T(8,128)}, f32[1,96,768]{2,1,0:T(8,128)}, f32[1,96,3072]{2,1,0:T(8,128)}, ...) | async-done | bytes 3538960 | tf_op jit(solution)/shard_map/psum | solution.py:222
  902.0 2.2 copy.72
  (187 shorter events, 21.4 us)
Async XLA Ops:
  7.2 5.8 copy-start.45
  7.3 6.0 copy-start.46
  7.3 46.0 %copy-start.39 = (bf16[1,384]{1,0:T(2,128)(2,1)S(1)}, bf16[1,384]{1,0:T(2,128)(2,1)}, u32[]{:S(2)}) copy-start(bf16[1,384]{1,0:T(2,128)(2,1)} %param.27) | copy-start | bytes 2308
  7.3 72.2 %copy-start.1 = (bf16[128,768]{1,0:T(8,128)(2,1)S(1)}, bf16[128,768]{1,0:T(8,128)(2,1)}, u32[]{:S(2)}) copy-start(bf16[128,768]{1,0:T(8,128)(2,1)} %param.15) | copy-start | bytes 589828
  7.3 72.5 %copy-start.37 = (s32[128]{0:T(128)S(1)}, s32[128]{0:T(128)}, u32[]{:S(2)}) copy-start(s32[128]{0:T(128)} %param.16) | copy-start | bytes 1540
  7.3 72.7 %all-gather.17.cloned.1.call-start = ((), (), s32[]{:S(2)}) async-start(), calls=%async_computation.8 | async-start | bytes 3981312 | tf_op jit(solution)/shard_map/all_gather | solution.py:269
  8.0 112.8 %all-gather.19.cloned.1.call-start = ((), (), s32[]{:S(2)}) async-start(), calls=%async_computation.9 | async-start | bytes 1327104 | tf_op jit(solution)/shard_map/all_gather | solution.py:271
  8.8 192.9 %all-gather.21.cloned.1.call-start = ((), (), s32[]{:S(2)}) async-start(), calls=%async_computation.10 | async-start | bytes 5308416 | tf_op jit(solution)/shard_map/all_gather | solution.py:275
  9.5 272.3 %all-gather.23.cloned.1.call-start = ((), (), s32[]{:S(2)}) async-start(), calls=%async_computation.11 | async-start | bytes 5308416 | tf_op jit(solution)/shard_map/all_gather | solution.py:277
  10.1 350.7 %reduce-scatter.7.cloned.1.call-start = ((), (), s32[]{:S(2)}) async-start(), calls=%async_computation.5 | async-start | bytes 2654208 | tf_op jit(solution)/shard_map/reduce_scatter | solution.py:213
  53.3 29.4 %copy-start.23 = (f32[768]{0:T(1024)}, f32[768]{0:T(1024)S(1)}, u32[]{:S(2)}) copy-start(f32[768]{0:T(1024)S(1)} %convert_element_type.137) | copy-start | bytes 9220
  79.4 122.3 %copy-start.21 = (f32[768]{0:T(1024)}, f32[768]{0:T(1024)S(1)}, u32[]{:S(2)}) copy-start(f32[768]{0:T(1024)S(1)} %convert_element_type.140) | copy-start | bytes 9220
  122.6 164.3 %copy-start.25 = (f32[128]{0:T(128)}, f32[128]{0:T(128)S(1)}, u32[]{:S(2)}) copy-start(f32[128]{0:T(128)S(1)} %broadcast_multiply_fusion.4) | copy-start | bytes 1540
  122.8 164.1 %copy-start.31 = (f32[128]{0:T(128)}, f32[128]{0:T(128)S(1)}, u32[]{:S(2)}) copy-start(f32[128]{0:T(128)S(1)} %add_rsqrt_fusion) | copy-start | bytes 1540
  201.7 80.1 %copy-start.17 = (bf16[128,768]{1,0:T(8,128)(2,1)S(1)}, bf16[128,768]{1,0:T(8,128)(2,1)}, u32[]{:S(2)}) copy-start(bf16[128,768]{1,0:T(8,128)(2,1)} %param.17) | copy-start | bytes 589828
  292.5 199.0 %reduce-scatter.5.cloned.1.call-start = ((), (), s32[]{:S(2)}) async-start(), calls=%async_computation.4 | async-start | bytes 7962624 | tf_op jit(solution)/shard_map/reduce_scatter | solution.py:211
  304.4 353.7 %reduce-scatter.9.cloned.1.call-start = ((), (), s32[]{:S(2)}) async-start(), calls=%async_computation.6 | async-start | bytes 10616832 | tf_op jit(solution)/shard_map/reduce_scatter | solution.py:217
  311.3 513.4 %reduce-scatter.11.cloned.1.call-start = ((), (), s32[]{:S(2)}) async-start(), calls=%async_computation.7 | async-start | bytes 10616832 | tf_op jit(solution)/shard_map/reduce_scatter | solution.py:219
  317.4 584.5 %all-reduce.21.cloned.1.call-start = ((), (), s32[]{:S(2)}) async-start(), calls=%async_computation.12 | async-start | bytes 7077888 | tf_op jit(solution)/shard_map/psum | solution.py:222
  824.7 8.2 copy-start.48
  824.7 8.2 copy-start.47
  824.7 8.2 copy-start.30
  824.7 8.2 copy-start.34
  824.7 9.1 copy-start.35
  (34 other events, 84.0 us)
Sparse Core Ops, SparseCore 0:
  10.3 68.5 all-gather.16
  81.1 39.6 all-gather.18
  123.0 78.6 all-gather.20
  203.7 78.0 all-gather.22
  292.6 67.2 reduce-scatter.6
  363.5 128.0 reduce-scatter.4
  495.5 162.4 reduce-scatter.8
  662.1 162.5 reduce-scatter.10
  827.4 74.4 all-reduce.20
where the time goes:
time: 914 us
  waiting for transfers between devices  723 us (79%)
  blocking collectives  109 us (12%)
  matrix products  45.5 us (5%)
  between operations  17.8 us (2%)
  local copies, waits for them, and re-layouts  13.4 us (1%)
    reduce_scatter x1, waiting for transfers between devices, own_grads(): lax.psum_scatter(gradients[10], 'shard', scatter_dimension=0, tiled=True)  167 us
    reduce_scatter x1, waiting for transfers between devices, own_grads(): lax.psum_scatter(gradients[8], 'shard', scatter_dimension=0, tiled=True)  167 us
    reduce_scatter x1, waiting for transfers between devices, own_grads(): lax.psum_scatter(gradients[2], 'shard', scatter_dimension=0, tiled=True)  131 us
    all_gather x1, waiting for transfers between devices, per_device(): lax.all_gather(fc_weight[layer_index], 'shard', axis=0, tiled=True)  78.9 us
    all_gather x1, waiting for transfers between devices, per_device(): lax.all_gather(proj_weight[layer_index], 'shard', axis=0, tiled=True)  76.8 us
    unnamed x2, blocking collectives  75.3 us
    psum x1, waiting for transfers between devices, own_grads(): lax.psum((shares[0], shares[1], shares[2], shares[3], shares[4], shares[5...  64.1 us
    all_gather x1, waiting for transfers between devices, per_device(): lax.all_gather(out_weight[layer_index], 'shard', axis=0, tiled=True)  36.8 us
  transfers between devices with their start and end apart: 9, of which 7 were waited for; matrix products, arithmetic and copies ran while one was open for 5% of the time, Pallas kernels for 0%

commit v1 on v0

--- a/solution.py
+++ b/solution.py
@@ -1,12 +1,55 @@
+import functools
 import jax
 import jax.numpy as jnp
 from jax import lax
 from jax.sharding import PartitionSpec as P
+from jax.lax import axis_index, axis_size, ppermute
 
 HEADS = 12
 HEAD = 64
 LAYERS = 1
 epsilon = 1e-05
+
+
+def serve_the_limits(block_in, axis_id, which_dim):
+    far_arr, current_value, mid_arr = (
+        axis_size(axis_id),
+        axis_index(axis_id),
+        block_in.shape[which_dim],
+    )
+    parts_seen = []
+    dev_i = 0
+    while dev_i < far_arr:
+        parts_seen.append((dev_i, (dev_i + 1) % far_arr))
+        dev_i += 1
+    block_list = []
+    dev_i = 0
+    while dev_i < far_arr:
+        block_list.append((dev_i, (dev_i - 1) % far_arr))
+        dev_i += 1
+    last = jnp.zeros(
+        (*block_in.shape[:which_dim], far_arr * mid_arr, *block_in.shape[which_dim + 1 :]),
+        block_in.dtype,
+    )
+    last = lax.dynamic_update_slice_in_dim(last, block_in, current_value * mid_arr, axis=which_dim)
+    side_arr = small = block_in
+    item_now = far_arr // 2
+    dev_j = 1
+    while dev_j < item_now + 1:
+        side_arr = ppermute(side_arr, perm=parts_seen, axis_name=axis_id)
+        last = lax.dynamic_update_slice_in_dim(
+            last, side_arr, (current_value - dev_j) % far_arr * mid_arr, axis=which_dim
+        )
+        if dev_j < far_arr - item_now:
+            small = ppermute(small, perm=block_list, axis_name=axis_id)
+            last = lax.dynamic_update_slice_in_dim(
+                last, small, (current_value + dev_j) % far_arr * mid_arr, axis=which_dim
+            )
+        dev_j = dev_j + 1
+    return last
+
+
+panels_answer = functools.partial(serve_the_limits, axis_id="shard", which_dim=0)
 
 
 def to_float(value):
@@ -274,7 +317,7 @@
         lax.all_gather(ln2_bias[layer_index], "shard", axis=0, tiled=True),
         lax.all_gather(fc_weight[layer_index], "shard", axis=0, tiled=True),
         lax.all_gather(fc_bias[layer_index], "shard", axis=0, tiled=True),
-        lax.all_gather(proj_weight[layer_index], "shard", axis=0, tiled=True),
+        panels_answer(proj_weight[layer_index]),
         lax.all_gather(proj_bias[layer_index], "shard", axis=0, tiled=True),
     )
     saved = layer_forward(residual, allowed, gathered, None)

time: 914 us -> 962 us (1.053)
  waiting for transfers between devices: 723 us -> 750 us
  starting transfers between devices: 0.54 us -> 16.7 us
    ppermute x0 -> x7, waiting for transfers between devices: none -> 86.8 us  [the longest x4 56.6 us: serve_the_limits(): side_arr = ppermute(side_arr, perm=parts_seen, axis_name=axis_id)]
    reduce_scatter x1, waiting for transfers between devices: 131 us -> 70.4 us  [own_grads(): lax.psum_scatter(gradients[2], 'shard', scatter_dimension=0, tiled=True)]
    ppermute x0 -> x7, starting transfers between devices: none -> 16.2 us  [the longest x3 13.1 us: serve_the_limits(): small = ppermute(small, perm=block_list, axis_name=axis_id)]
  transfers between devices with their start and end apart: 9 -> 16, of which waited for: 7 -> 13; matrix products, arithmetic and copies ran while one was open for 5% -> 5% of each run, Pallas kernels for 0% -> 0%
where the time goes in v1:
time: 962 us; the launch traced here: 961 us
  waiting for transfers between devices  750 us (78%)
  blocking collectives  111 us (12%)
  matrix products  42.9 us (4%)
  local copies, waits for them, and re-layouts  19.4 us (2%)
  between operations  17.9 us (2%)
  starting transfers between devices  16.7 us (2%)
    reduce_scatter x1, waiting for transfers between devices, own_grads(): lax.psum_scatter(gradients[10], 'shard', scatter_dimension=0, tiled=True)  166 us
    reduce_scatter x1, waiting for transfers between devices, own_grads(): lax.psum_scatter(gradients[8], 'shard', scatter_dimension=0, tiled=True)  166 us
    all_gather x1, waiting for transfers between devices, per_device(): lax.all_gather(fc_weight[layer_index], 'shard', axis=0, tiled=True)  78.9 us
    unnamed x2, blocking collectives  77.8 us
    all_gather x1, waiting for transfers between devices, per_device(): lax.all_gather(proj_weight[layer_index], 'shard', axis=0, tiled=True)  76.8 us
    reduce_scatter x1, waiting for transfers between devices, own_grads(): lax.psum_scatter(gradients[2], 'shard', scatter_dimension=0, tiled=True)  70.4 us
    psum x1, waiting for transfers between devices, own_grads(): lax.psum((shares[0], shares[1], shares[2], shares[3], shares[4], shares[5...  64.2 us
    ppermute x4, waiting for transfers between devices, serve_the_limits(): side_arr = ppermute(side_arr, perm=parts_seen, axis_name=axis_id)  56.6 us
  transfers between devices with their start and end apart: 16, of which 13 were waited for; matrix products, arithmetic and copies ran while one was open for 5% of the time, Pallas kernels for 0%

profile of v1, /device:TPU:0, one launch (start us, length us, event | category | flops | bytes accessed | tf_op | source)
XLA Modules:
  0.0 961.4 jit_solution(3826830733126293712)
XLA Ops:
  13.7 39.5 %all-reduce.18 = (bf16[1536]{0:T(1024)(128)(2,1)S(1)}, bf16[768]{0:T(1024)(128)(2,1)S(1)}, bf16[768]{0:T(1024)(128)(2,1)S(1)}, bf16[768]{0:T(1024)(128)(2,1)S(1)...) all-reduce(bf16[1536]{0:T(1024)(128)(2,1)S(1)} %dynamic-update-slic, ...), channel_id=5, replica_groups=mesh['rep'=4,'shard'=8] {'shard'}, use_global_device_ids=true, to_apply=%add.2 | all-reduce | flops 6144 | bytes 24576
  53.3 26.1 %all-gather.9 = bf16[1,3072]{1,0:T(2,128)(2,1)S(1)} all-gather(bf16[1,384]{1,0:T(2,128)(2,1)S(1)} %copy-done.47), channel_id=11, replica_groups=mesh['rep'=4,'shard'=8] {'shard'}, dimensions={1}, use_global_device_ids=true | all-gather | bytes 6912 | tf_op jit(solution)/shard_map/all_gather | solution.py:319
  84.0 36.7 %all-gather.19.cloned.1.call-done = bf16[1,768,768]{2,1,0:T(8,128)(2,1)} async-done(((bf16[1,96,768]{2,1,0:T(8,128)(2,1)}), bf16[1,768,768]{2,1,0:T(8,128)(2,1)}) %all-gather.19.cloned.1.call-update) | async-done | bytes 1179664 | tf_op jit(solution)/shard_map/all_gather | solution.py:314
  122.7 78.9 %all-gather.21.cloned.1.call-done = bf16[1,768,3072]{2,1,0:T(8,128)(2,1)} async-done(((bf16[1,96,3072]{2,1,0:T(8,128)(2,1)}), bf16[1,768,3072]{2,1,0:T(8,128)(2,1)}) %all-gather.21.cloned.1.call-update) | async-done | bytes 4718608 | tf_op jit(solution)/shard_map/all_gather | solution.py:318
  204.9 76.8 %all-gather.23.cloned.1.call-done = bf16[1,3072,768]{2,1,0:T(8,128)(2,1)} async-done(((bf16[1,384,768]{2,1,0:T(8,128)(2,1)}), bf16[1,3072,768]{2,1,0:T(8,128)(2,1)}) %all-gather.23.cloned.1.call-update) | async-done | bytes 4718608 | tf_op jit(solution)/shard_map/all_gather | solution.py:342
  281.8 5.0 convert_reduce_fusion
  300.2 4.1 fusion.57
  305.5 5.8 fusion.60
  312.2 5.2 fusion.61
  319.0 4.2 collective-permute-start.1
  323.2 26.4 %collective-permute-done = bf16[384,768]{1,0:T(8,128)(2,1)S(1)} collective-permute-done((bf16[384,768]{1,0:T(8,128)(2,1)S(1)}, bf16[384,768]{1,0:T(8,128)(2,1)S(1)}, u32[]{:S(2)}, u32[]{:S(2)}) %collective-permute-start) | collective-permute-done | bytes 589856 | tf_op jit(solution)/shard_map/ppermute | solution.py:39
  354.9 12.2 %collective-permute-done.2 = bf16[384,768]{1,0:T(8,128)(2,1)} collective-permute-done((bf16[384,768]{1,0:T(8,128)(2,1)S(1)}, bf16[384,768]{1,0:T(8,128)(2,1)}, u32[]{:S(2)}, u32[]{:S(2)}) %collective-permute-start.2) | collective-permute-done | bytes 589856 | tf_op jit(solution)/shard_map/ppermute | solution.py:39
  369.5 11.4 %collective-permute-done.3 = bf16[384,768]{1,0:T(8,128)(2,1)} collective-permute-done((bf16[384,768]{1,0:T(8,128)(2,1)}, bf16[384,768]{1,0:T(8,128)(2,1)}, u32[]{:S(2)}, u32[]{:S(2)}) %collective-permute-start.3) | collective-permute-done | bytes 589856 | tf_op jit(solution)/shard_map/ppermute | solution.py:44
  380.9 6.1 collective-permute-start.5
  387.1 13.6 %collective-permute-done.4 = bf16[384,768]{1,0:T(8,128)(2,1)} collective-permute-done((bf16[384,768]{1,0:T(8,128)(2,1)}, bf16[384,768]{1,0:T(8,128)(2,1)}, u32[]{:S(2)}, u32[]{:S(2)}) %collective-permute-start.4) | collective-permute-done | bytes 589856 | tf_op jit(solution)/shard_map/ppermute | solution.py:39
  405.4 18.8 %collective-permute-done.5 = bf16[384,768]{1,0:T(8,128)(2,1)S(1)} collective-permute-done((bf16[384,768]{1,0:T(8,128)(2,1)}, bf16[384,768]{1,0:T(8,128)(2,1)S(1)}, u32[]{:S(2)}, u32[]{:S(2)}) %collective-permute-start.5) | collective-permute-done | bytes 589856 | tf_op jit(solution)/shard_map/ppermute | solution.py:44
  424.2 4.5 collective-permute-done.6
  431.0 38.2 %all-reduce.15 = (f32[768]{0:T(1024)S(1)}, f32[768]{0:T(1024)S(1)}, f32[1536]{0:T(1024)S(1)}, f32[768]{0:T(1024)S(1)}, f32[768]{0:T(1024)S(1)}, /*index=5*/f32[7...) all-reduce(f32[768]{0:T(1024)S(1)} %get-tuple-element.16, ...), channel_id=14, replica_groups=mesh['rep'=4,'shard'=8] {'shard'}, use_global_device_ids=true, to_apply=%region_12.13.clone | all-reduce | flops 9216 | bytes 73728
  469.3 70.4 %reduce-scatter.5.cloned.1.call-done = f32[96,2304]{1,0:T(8,128)} async-done(((f32[768,2304]{1,0:T(8,128)}), f32[96,2304]{1,0:T(8,128)}) %reduce-scatter.5.cloned.1.call-update) | async-done | bytes 884752 | tf_op jit(solution)/shard_map/reduce_scatter | solution.py:254
  539.7 166.4 %reduce-scatter.9.cloned.1.call-done = f32[96,3072]{1,0:T(8,128)} async-done(((f32[768,3072]{1,0:T(8,128)}), f32[96,3072]{1,0:T(8,128)}) %reduce-scatter.9.cloned.1.call-update) | async-done | bytes 1179664 | tf_op jit(solution)/shard_map/reduce_scatter | solution.py:260
  706.1 166.5 %reduce-scatter.11.cloned.1.call-done = f32[384,768]{1,0:T(8,128)} async-done(((f32[3072,768]{1,0:T(8,128)}), f32[384,768]{1,0:T(8,128)}) %reduce-scatter.11.cloned.1.call-update) | async-done | bytes 1179664 | tf_op jit(solution)/shard_map/reduce_scatter | solution.py:262
  873.2 7.5 all-reduce.16
  881.6 4.1 fusion.28
  885.6 64.2 %all-reduce.21.cloned.1.call-done = (f32[1,96,2304]{2,1,0:T(8,128)}, f32[1,96,768]{2,1,0:T(8,128)}, f32[1,96,3072]{2,1,0:T(8,128)}, f32[1,384,768]{2,1,0:T(8,128)}) async-done(((f32[1,96,2304]{2,1,0:T(8,128)}, f32[1,96,768]{2,1,0:T(8,128)}, f32[1,96,3072]{2,1,0:T(8,128)}, f32[1,384,768]{2,1,0:T(8,128)}), (f32[1,96,2304]{2,1,0:T(8,128)}, f32[1,96,768]{2,1,0:T(8,128)}, f32[1,96,3072]{2,1,0:T(8,128)}, ...) | async-done | bytes 3538960 | tf_op jit(solution)/shard_map/psum | solution.py:265
  (222 shorter events, 50.8 us)
Async XLA Ops:
  7.3 46.1 %copy-start.47 = (bf16[1,384]{1,0:T(2,128)(2,1)S(1)}, bf16[1,384]{1,0:T(2,128)(2,1)}, u32[]{:S(2)}) copy-start(bf16[1,384]{1,0:T(2,128)(2,1)} %param.27) | copy-start | bytes 2308
  7.3 72.2 %copy-start.1 = (bf16[128,768]{1,0:T(8,128)(2,1)S(1)}, bf16[128,768]{1,0:T(8,128)(2,1)}, u32[]{:S(2)}) copy-start(bf16[128,768]{1,0:T(8,128)(2,1)} %param.15) | copy-start | bytes 589828
  7.3 72.6 %copy-start.45 = (s32[128]{0:T(128)S(1)}, s32[128]{0:T(128)}, u32[]{:S(2)}) copy-start(s32[128]{0:T(128)} %param.16) | copy-start | bytes 1540
  7.3 72.7 %all-gather.17.cloned.1.call-start = ((), (), s32[]{:S(2)}) async-start(), calls=%async_computation.8 | async-start | bytes 3981312 | tf_op jit(solution)/shard_map/all_gather | solution.py:312
  8.0 112.8 %all-gather.19.cloned.1.call-start = ((), (), s32[]{:S(2)}) async-start(), calls=%async_computation.9 | async-start | bytes 1327104 | tf_op jit(solution)/shard_map/all_gather | solution.py:314
  8.8 192.9 %all-gather.21.cloned.1.call-start = ((), (), s32[]{:S(2)}) async-start(), calls=%async_computation.10 | async-start | bytes 5308416 | tf_op jit(solution)/shard_map/all_gather | solution.py:318
  9.5 272.2 %all-gather.23.cloned.1.call-start = ((), (), s32[]{:S(2)}) async-start(), calls=%async_computation.11 | async-start | bytes 5308416 | tf_op jit(solution)/shard_map/all_gather | solution.py:342
  10.1 459.2 %reduce-scatter.7.cloned.1.call-start = ((), (), s32[]{:S(2)}) async-start(), calls=%async_computation.5 | async-start | bytes 2654208 | tf_op jit(solution)/shard_map/reduce_scatter | solution.py:256
  79.4 122.3 %copy-start.26 = (f32[768]{0:T(1024)}, f32[768]{0:T(1024)S(1)}, u32[]{:S(2)}) copy-start(f32[768]{0:T(1024)S(1)} %convert_element_type.140) | copy-start | bytes 9220
  122.5 164.3 %copy-start.30 = (f32[128]{0:T(128)}, f32[128]{0:T(128)S(1)}, u32[]{:S(2)}) copy-start(f32[128]{0:T(128)S(1)} %broadcast_multiply_fusion.4) | copy-start | bytes 1540
  122.7 164.1 %copy-start.39 = (f32[128]{0:T(128)}, f32[128]{0:T(128)S(1)}, u32[]{:S(2)}) copy-start(f32[128]{0:T(128)S(1)} %add_rsqrt_fusion) | copy-start | bytes 1540
  201.7 80.1 %copy-start.20 = (bf16[128,768]{1,0:T(8,128)(2,1)S(1)}, bf16[128,768]{1,0:T(8,128)(2,1)}, u32[]{:S(2)}) copy-start(bf16[128,768]{1,0:T(8,128)(2,1)} %param.17) | copy-start | bytes 589828
  292.5 247.2 %reduce-scatter.5.cloned.1.call-start = ((), (), s32[]{:S(2)}) async-start(), calls=%async_computation.4 | async-start | bytes 7962624 | tf_op jit(solution)/shard_map/reduce_scatter | solution.py:254
  304.4 401.7 %reduce-scatter.9.cloned.1.call-start = ((), (), s32[]{:S(2)}) async-start(), calls=%async_computation.6 | async-start | bytes 10616832 | tf_op jit(solution)/shard_map/reduce_scatter | solution.py:260
  311.3 561.2 %reduce-scatter.11.cloned.1.call-start = ((), (), s32[]{:S(2)}) async-start(), calls=%async_computation.7 | async-start | bytes 10616832 | tf_op jit(solution)/shard_map/reduce_scatter | solution.py:262
  317.4 49.7 %copy-start.44 = (bf16[768]{0:T(1024)(128)(2,1)S(1)}, bf16[768]{0:T(1024)(128)(2,1)}, u32[]{:S(2)}) copy-start(bf16[768]{0:T(1024)(128)(2,1)} %get-tuple-element.48) | copy-start | bytes 4612
  317.5 632.4 %all-reduce.21.cloned.1.call-start = ((), (), s32[]{:S(2)}) async-start(), calls=%async_computation.12 | async-start | bytes 7077888 | tf_op jit(solution)/shard_map/psum | solution.py:265
  318.5 31.1 %collective-permute-start = (bf16[384,768]{1,0:T(8,128)(2,1)S(1)}, bf16[384,768]{1,0:T(8,128)(2,1)S(1)}, u32[]{:S(2)}, u32[]{:S(2)}) collective-permute-start(bf16[384,768]{1,0:T(8,128)(2,1)S(1)} %bitcast.94), channel_id=1, source_target_pairs={{0,1},{1,2},{2,3},{3,4},{4,5},{5,6},{6,7},{7,0},{8,9},{9,10},{10,1... | collective-permute-start | bytes 1769480 | tf_op jit(solution)/shard_map/ppermute | solution.py:39
  319.0 33.1 %collective-permute-start.1 = (bf16[384,768]{1,0:T(8,128)(2,1)S(1)}, bf16[384,768]{1,0:T(8,128)(2,1)}, u32[]{:S(2)}, u32[]{:S(2)}) collective-permute-start(bf16[384,768]{1,0:T(8,128)(2,1)S(1)} %bitcast.95), channel_id=1, source_target_pairs={{0,7},{1,0},{2,1},{3,2},{4,3},{5,4},{6,5},{7,6},{8,15},{9,8},{10,9... | collective-permute-start | bytes 1769480 | tf_op jit(solution)/shard_map/ppermute | solution.py:44
  349.6 17.5 %collective-permute-start.2 = (bf16[384,768]{1,0:T(8,128)(2,1)S(1)}, bf16[384,768]{1,0:T(8,128)(2,1)}, u32[]{:S(2)}, u32[]{:S(2)}) collective-permute-start(bf16[384,768]{1,0:T(8,128)(2,1)S(1)} %collective-permute-done), channel_id=1, source_target_pairs={{0,1},{1,2},{2,3},{3,4},{4,5},{5,6},{6,7},{7,0},{8,9},{9,10},{10,1... | collective-permute-start | bytes 1769480 | tf_op jit(solution)/shard_map/ppermute | solution.py:39
  352.1 28.8 %collective-permute-start.3 = (bf16[384,768]{1,0:T(8,128)(2,1)}, bf16[384,768]{1,0:T(8,128)(2,1)}, u32[]{:S(2)}, u32[]{:S(2)}) collective-permute-start(bf16[384,768]{1,0:T(8,128)(2,1)} %collective-permute-done.1), channel_id=1, source_target_pairs={{0,7},{1,0},{2,1},{3,2},{4,3},{5,4},{6,5},{7,6},{8,15},{9,8},{10,9... | collective-permute-start | bytes 1769480 | tf_op jit(solution)/shard_map/ppermute | solution.py:44
  367.1 33.5 %collective-permute-start.4 = (bf16[384,768]{1,0:T(8,128)(2,1)}, bf16[384,768]{1,0:T(8,128)(2,1)}, u32[]{:S(2)}, u32[]{:S(2)}) collective-permute-start(bf16[384,768]{1,0:T(8,128)(2,1)} %collective-permute-done.2), channel_id=1, source_target_pairs={{0,1},{1,2},{2,3},{3,4},{4,5},{5,6},{6,7},{7,0},{8,9},{9,10},{10,1... | collective-permute-start | bytes 1769480 | tf_op jit(solution)/shard_map/ppermute | solution.py:39
  380.9 43.3 %collective-permute-start.5 = (bf16[384,768]{1,0:T(8,128)(2,1)}, bf16[384,768]{1,0:T(8,128)(2,1)S(1)}, u32[]{:S(2)}, u32[]{:S(2)}) collective-permute-start(bf16[384,768]{1,0:T(8,128)(2,1)} %collective-permute-done.3), channel_id=1, source_target_pairs={{0,7},{1,0},{2,1},{3,2},{4,3},{5,4},{6,5},{7,6},{8,15},{9,8},{10,9... | collective-permute-start | bytes 1769480 | tf_op jit(solution)/shard_map/ppermute | solution.py:44
  400.6 28.0 %collective-permute-start.6 = (bf16[384,768]{1,0:T(8,128)(2,1)}, bf16[384,768]{1,0:T(8,128)(2,1)S(1)}, u32[]{:S(2)}, u32[]{:S(2)}) collective-permute-start(bf16[384,768]{1,0:T(8,128)(2,1)} %collective-permute-done.4), channel_id=1, source_target_pairs={{0,1},{1,2},{2,3},{3,4},{4,5},{5,6},{6,7},{7,0},{8,9},{9,10},{10,1... | collective-permute-start | bytes 1769480 | tf_op jit(solution)/shard_map/ppermute | solution.py:39
  (47 other events, 271.3 us)
Sparse Core Ops, SparseCore 0:
  10.3 68.5 all-gather.16
  81.1 39.6 all-gather.18
  123.0 78.6 all-gather.20
  203.7 78.0 all-gather.22
  292.6 103.3 reduce-scatter.6
  399.6 140.0 reduce-scatter.4
  543.7 162.3 reduce-scatter.8
  710.1 162.4 reduce-scatter.10
  875.3 74.4 all-reduce.20
